TPU v7x, 256 devices: a whole 4x4x8 slice. The times are simulated.
256 devices in a mesh: scen: 16 (over z, core), clus: 16 (over y, x).
Axes of the slice: x: 4, y: 4, z: 8, core: 2. Of those that a mesh axis runs over, the one named last changes fastest.
Arguments:
- duals: bfloat16 [16384, 2, 128], P(('scen', 'clus')), may hold values from -6 to 6
- blocks: bfloat16 [16384, 2, 128, 128], P(('scen', 'clus')), may hold values from -0.5 to 0.5
- prob: float32 [16384], P(('scen', 'clus')), may hold values from 0.25 to 4
- cluster_map: int32 [16384], P(('scen', 'clus')), may hold values from 0 to 15
- block_cols: int32 [16384, 2], P(('scen', 'clus')), may hold values from 0 to 255
- counts: int32 [256], P(('scen', 'clus')), may hold values from 16 to 64, as said below
- cut_owner_rows: int32 [256], replicated, may hold values from 0 to 255, as said below
Outputs:
- master_cuts: float32 [256, 32768], P('clus', 'scen')
Inputs may be any that keep to these rules, and one draw needn't show every extreme that they name: counts of live slots, one device holding 64 live slots in every draw. A permutation of the master cut rows; of the cuts k = i * 16 to (i + 1) * 16 - 1 at most 1 have cut_owner_rows[k] in e * 16 to (e + 1) * 16 - 1, for any i and e, and 1 is reached.
All inputs are finite; a program needn't handle non-finite values.
Results may differ from a plain program's by a relative error of at most 0.0029.
Values sent between devices are 32-bit elements; how exact they have to be, the bound alone decides.
A program may use at most 64 MiB of HBM per device.

v0:
```python
import jax
import jax.numpy as jnp
from jax import lax
from jax.sharding import PartitionSpec as P

N1 = 32768
KC = 16


def body(duals, blocks, prob, cluster_map, block_cols, counts, cut_owner_rows):
    slots = prob.shape[0]
    width = blocks.shape[-1]
    col_blocks = N1 // width
    cluster_position = lax.axis_index("clus")
    own_blocks = col_blocks // lax.axis_size("scen")
    columns = own_blocks * width
    live = jnp.arange(slots, dtype=jnp.int32) < counts[0]
    weight = jnp.where(live, prob, jnp.float32(0.0))
    weighted_duals = (weight[:, None, None] * duals.astype(jnp.float32)).astype(jnp.bfloat16)
    dual_products = jnp.einsum(
        "plqv,plq->plv", blocks, weighted_duals, preferred_element_type=jnp.float32
    )
    dual_products = dual_products.reshape(-1, width)
    keys = (cluster_map[:, None] * col_blocks + block_cols).reshape(-1)
    clus_part = keys // col_blocks
    col_part = keys % col_blocks
    valid = (col_part >= 0) & (col_part < lax.axis_size("scen") * own_blocks)
    target = jnp.where(valid, col_part * KC + clus_part, -1)
    onehot = (
        target[None, :]
        == jnp.arange(lax.axis_size("scen") * own_blocks * KC, dtype=jnp.int32)[:, None]
    ).astype(jnp.float32)
    summed = jnp.dot(
        onehot, dual_products, precision=lax.Precision.HIGHEST, preferred_element_type=jnp.float32
    )
    probability_shares = lax.psum_scatter(
        summed.reshape(lax.axis_size("scen") * own_blocks, KC, width),
        "scen",
        scatter_dimension=0,
        tiled=True,
    )
    reduced = jnp.transpose(probability_shares, (1, 0, 2)).reshape(KC, columns)
    owners = cut_owner_rows - cluster_position * KC
    onehot = (owners[None, :] == jnp.arange(KC, dtype=jnp.int32)[:, None]).astype(jnp.float32)
    return jnp.dot(
        onehot,
        lax.all_gather(reduced, "clus", axis=0, tiled=True),
        precision=lax.Precision.HIGHEST,
        preferred_element_type=jnp.float32,
    )


def solution(mesh):
    placed = (
        P(("scen", "clus"), None, None),
        P(("scen", "clus"), None, None, None),
        P(("scen", "clus")),
        P(("scen", "clus")),
        P(("scen", "clus"), None),
        P(("scen", "clus")),
        P(),
    )
    return jax.shard_map(
        body, mesh=mesh, in_specs=placed, out_specs=P("clus", "scen"), check_vma=False
    )
```

profile of v0, /device:TPU:1, one launch (start us, length us, event | category | flops | bytes accessed | tf_op | source)
XLA Modules:
  0.0 139.5 jit_solution(1167170672462910426)
XLA Ops:
  6.5 0.0 reduce-scatter.2.cloned.1.call-start
  7.2 0.7 broadcast_multiply_fusion
  7.9 0.7 broadcast_add_fusion
  8.5 0.1 copy.9
  8.6 0.1 reshape.86
  8.8 0.7 compare_select_fusion
  9.5 0.9 fusion.6
  10.3 3.4 %fusion.4 = f32[64,2,1,128]{3,2,1,0:T(1,128)S(1)} fusion(bf16[64,2,128,128]{3,2,1,0:T(8,128)(2,1)} %param.8, bf16[64,2,128,1]{2,1,0,3:T(2,128)(2,1)S(1)} %fusion.6), kind=kOutput, calls=%fused_computation.5 | convolution fusion | flops 4194304 | bytes 4292608 | tf_op jit(solution)/shard_map/plqv,plq->plv/dot_general | solution.py:20
  13.7 0.0 copy-start
  13.7 2.5 %fusion = f32[256,16,128]{2,0,1:T(8,128)} fusion(f32[128,128,1]{1,0,2:T(8,128)S(1)} %bitcast.19, s32[256,16]{0,1:T(8,128)S(1)} %multiply_add_fusion, s32[128]{0:T(128)S(1)} %and_select_fusion.1), kind=kOutput, calls=%fused_computation | convolution fusion | flops 805830656 | bytes 2179584 | tf_op jit(solution)/shard_map/dot_general | solution.py:33
  16.2 0.0 reduce-scatter.2.cloned.1.call-update
  16.3 0.0 all-gather.2.cloned.1.call-start
  16.3 60.2 %reduce-scatter.2.cloned.1.call-done = f32[16,16,128]{2,0,1:T(8,128)} async-done(((f32[256,16,128]{2,0,1:T(8,128)}), f32[16,16,128]{2,0,1:T(8,128)}) %reduce-scatter.2.cloned.1.call-update) | async-done | bytes 131088 | tf_op jit(solution)/shard_map/reduce_scatter | solution.py:36
  76.6 1.6 %copy.16 = f32[2,8,16,128]{3,1,2,0:T(8,128)} copy(f32[2,8,16,128]{3,2,1,0:T(8,128)} %bitcast.20) | data formatting | bytes 262144
  78.2 0.0 all-gather.2.cloned.1.call-update
  78.2 0.0 copy-done
  78.2 51.4 %all-gather.2.cloned.1.call-done = f32[256,2048]{1,0:T(8,128)} async-done(((f32[16,2048]{1,0:T(8,128)}), f32[256,2048]{1,0:T(8,128)}) %all-gather.2.cloned.1.call-update) | async-done | bytes 2097168 | tf_op jit(solution)/shard_map/all_gather | solution.py:47
  129.6 3.0 %fusion.7 = f32[16,2048]{1,0:T(8,128)} fusion(f32[256,2048]{1,0:T(8,128)} %all-gather.2.cloned.1.call-done, s32[256]{0:T(256)S(1)} %broadcast_subtract_fusion), kind=kOutput, calls=%fused_computation.11 | convolution fusion | flops 100667392 | bytes 2229248 | tf_op jit(solution)/shard_map/dot_general | solution.py:45
  (3 shorter events, 0.0 us)
Async XLA Ops:
  6.5 70.0 %reduce-scatter.2.cloned.1.call-start = ((), (), s32[]{:S(2)}) async-start(), calls=%async_computation.1 | async-start | bytes 2228224 | tf_op jit(solution)/shard_map/reduce_scatter | solution.py:36
  13.7 64.5 %copy-start = (s32[256]{0:T(256)S(1)}, s32[256]{0:T(256)}, u32[]{:S(2)}) copy-start(s32[256]{0:T(256)} %param.13) | copy-start | bytes 3076
  16.3 113.3 %all-gather.2.cloned.1.call-start = ((), (), s32[]{:S(2)}) async-start(), calls=%async_computation.2 | async-start | bytes 2228224 | tf_op jit(solution)/shard_map/all_gather | solution.py:47
Sparse Core Ops, SparseCore 0:
  16.4 60.1 reduce-scatter.1
  79.0 50.5 all-gather.1
where the time goes:
time: 140 us; the launch traced here: 139 us
  waiting for transfers between devices  112 us (80%)
  between operations  14.1 us (10%)
  matrix products  8.91 us (6%)
  other arithmetic  2.91 us (2%)
  local copies, waits for them, and re-layouts  1.84 us (1%)
    reduce_scatter x1, waiting for transfers between devices, body(): lax.psum_scatter(summed.reshape(lax.axis_size('scen') * own_blocks, KC, w...  60.2 us
    all_gather x1, waiting for transfers between devices, body(): lax.all_gather(reduced, 'clus', axis=0, tiled=True)  51.4 us
    dot_general x1, matrix products, body(): jnp.einsum('plqv,plq->plv', blocks, weighted_duals, preferred_element_typ...  3.37 us
    dot_general x1, matrix products, body(): jnp.dot(onehot, lax.all_gather(reduced, 'clus', axis=0, tiled=True), prec...  3.02 us
  transfers between devices with their start and end apart: 2, of which 2 were waited for; matrix products, arithmetic and copies ran while one was open for 0% of the time, Pallas kernels for 0%

commit v1 on v0

v1 whole, which is shorter than its diff:
```python
import functools

import jax
import jax.numpy as jnp
from jax import lax
from jax.experimental import pallas as pl
from jax.experimental.pallas import tpu as pltpu
from jax.sharding import PartitionSpec as P

N1 = 32768
KC = 16
BLK = 128
ROWS = 128
SCEN = 16
CLUS = 16
OWN = 16
PIECE = 136
CHUNKS = ((96, 40), (64, 32), (32, 32), (0, 32))
MESH = pl.DeviceIdType.MESH
F32, BF16, I32 = jnp.float32, jnp.bfloat16, jnp.int32


def travels(direction, hop, chunk):
    return hop <= 3 or (hop == 4 and (chunk < 2) == (direction == 0))


def kernel(
    duals_h, blocks_h, prob_h, cmap_h, cols_h, counts_h, owners_h, owners2_h, out,
    blk, dua, prb, cmp, col, cnt, own, ownv, inv_v, inv_s, pieces, total, landed,
    small_sem, blk_sem, ring_send, ring_recv, sib_send, sib_recv, row_send, row_recv,
):
    s, i = lax.axis_index("scen"), lax.axis_index("clus")
    right, left, sibling = (s + 2) % SCEN, (s + SCEN - 2) % SCEN, s + 1 - 2 * (s % 2)
    nc = len(CHUNKS)

    smalls = [
        pltpu.make_async_copy(src, dst, small_sem.at[n])
        for n, (src, dst) in enumerate(
            ((counts_h, cnt), (owners_h, own), (prob_h, prb), (duals_h, dua), (cmap_h, cmp), (cols_h, col), (owners2_h, ownv))
        )
    ]
    for c in smalls:
        c.start()
    loads = []
    for n, (lo, rows) in enumerate(CHUNKS):
        c = pltpu.make_async_copy(blocks_h.at[pl.ds(lo, 32)], blk.at[pl.ds(lo, 32)], blk_sem.at[n])
        c.start()
        loads.append(c)

    barrier = pltpu.get_barrier_semaphore()
    for dev in (right, left, sibling):
        pl.semaphore_signal(barrier, inc=1, device_id=(dev, i), device_id_type=MESH)
    for k in range(1, CLUS):
        pl.semaphore_signal(barrier, inc=1, device_id=(s, (i + k) % CLUS), device_id_type=MESH)

    for c in smalls:
        c.wait()

    lane64 = lax.broadcasted_iota(I32, (1, 64), 1)
    weight = jnp.where(lane64 < cnt[0], prb[...], 0.0)
    spread = (lax.broadcasted_iota(I32, (ROWS, 64), 0) // 2) == lax.broadcasted_iota(I32, (ROWS, 64), 1)
    weight_col = jnp.sum(jnp.where(spread, weight, 0.0), axis=1, keepdims=True)
    weighted = (weight_col * dua[...].astype(F32)).astype(BF16).astype(F32)

    pick = (
        lax.broadcasted_iota(I32, (64, ROWS), 0) == lax.broadcasted_iota(I32, (64, ROWS), 1) // 2
    ).astype(F32).astype(BF16)
    both = jnp.dot(col[...].astype(F32).astype(BF16), pick, preferred_element_type=F32)
    cluster = jnp.dot(cmp[...].astype(F32).astype(BF16), pick, preferred_element_type=F32)
    lane = lax.broadcasted_iota(I32, (1, ROWS), 1)
    column = jnp.where(lane % 2 == 0, both[0:1], both[1:2])
    dest = jnp.zeros((1, ROWS), I32)
    cluster = cluster.astype(I32)
    for c in range(KC):
        dest = jnp.where(cluster == c, own[i * KC + c] // KC, dest)
    keys = dest.astype(F32) * 256.0 + column
    pieces[s, pl.ds(ROWS, 8), :] = jnp.broadcast_to(keys, (8, ROWS))

    def ring_copy(direction, hop, n):
        lo, rows = CHUNKS[n]
        source = (s + (SCEN - 2 * (hop - 1) if direction == 0 else 2 * (hop - 1))) % SCEN
        ref = pieces.at[source, pl.ds(lo, rows), :]
        return pltpu.make_async_remote_copy(
            src_ref=ref, dst_ref=ref,
            send_sem=ring_send.at[direction, hop - 1, n], recv_sem=ring_recv.at[direction, hop - 1, n],
            device_id=(right if direction == 0 else left, i), device_id_type=MESH,
        )

    def sib_copy(direction, hop, n):
        lo, rows = CHUNKS[n]
        source = (s + (SCEN - 2 * hop if direction == 0 else 2 * hop)) % SCEN
        ref = pieces.at[source, pl.ds(lo, rows), :]
        return pltpu.make_async_remote_copy(
            src_ref=ref, dst_ref=ref,
            send_sem=sib_send.at[direction, hop, n], recv_sem=sib_recv.at[direction, hop, n],
            device_id=(sibling, i), device_id_type=MESH,
        )

    started = []

    def start(copy):
        copy.start()
        started.append(copy)

    sub = lax.broadcasted_iota(I32, (8, BLK), 0)
    for n, (lo, rows) in enumerate(CHUNKS):
        loads[n].wait()
        for t in range(4):
            at = lo + 8 * t
            w = weighted[at : at + 8]
            lhs = jnp.concatenate([jnp.where(sub == g, w, 0.0) for g in range(8)], axis=1).astype(BF16)
            rhs = blk[at : at + 8].reshape(8 * BLK, BLK)
            pieces[s, pl.ds(at, 8), :] = jnp.dot(lhs, rhs, preferred_element_type=F32)
        if n == 0:
            pl.semaphore_wait(barrier, 3 + CLUS - 1)
        start(ring_copy(0, 1, n))
        start(ring_copy(1, 1, n))
        start(sib_copy(0, 0, n))

    total[...] = jnp.zeros_like(total)
    target = lax.broadcasted_iota(I32, (CLUS * OWN, ROWS), 0)

    def hot(source):
        key = pieces[source, pl.ds(ROWS, 1), :].astype(I32)
        cb = key % 256 - s * OWN
        t = jnp.where((cb >= 0) & (cb < OWN), key // 256 * OWN + cb, -1)
        return (target == t).astype(F32).astype(BF16)

    def add(first, second):
        onehot = jnp.concatenate([hot(first), hot(second)], axis=1)
        p = jnp.concatenate([pieces[first, pl.ds(0, ROWS), :], pieces[second, pl.ds(0, ROWS), :]], axis=0)
        high = p.astype(BF16)
        low = (p - high.astype(F32)).astype(BF16)
        total[...] += jnp.dot(onehot, high, preferred_element_type=F32) + jnp.dot(
            onehot, low, preferred_element_type=F32
        )

    def place(direction, hop, of=None):
        of = s if of is None else of
        return (of + (SCEN - 2 * hop if direction == 0 else 2 * hop)) % SCEN

    def add_hop(direction, hop):
        for n in range(nc):
            sib_copy(direction, hop, n).wait_recv()
        add(place(direction, hop), place(direction, hop, sibling))

    lane256 = lax.broadcasted_iota(I32, (16, 256), 1)
    row16 = lax.broadcasted_iota(I32, (16, 256), 0)
    ownrow = ownv[...]
    inv_col = jnp.max(jnp.where(ownrow == i * KC + row16, lane256 // KC, 0), axis=1, keepdims=True)
    inv_v[...] = jnp.broadcast_to(inv_col, (16, 128))
    c = pltpu.make_async_copy(inv_v, inv_s, small_sem.at[0])
    c.start()
    c.wait()

    for hop in range(1, 5):
        for n in range(nc):
            for direction in (0, 1):
                if travels(direction, hop, n):
                    ring_copy(direction, hop, n).wait_recv()
                    if travels(direction, hop + 1, n):
                        start(ring_copy(direction, hop + 1, n))
                    start(sib_copy(direction, hop, n))
            if n == 1:
                if hop == 1:
                    add_hop(0, 0)
                else:
                    add_hop(0, hop - 1)
            if n == 3 and hop > 1:
                add_hop(1, hop - 1)
    for n in range(nc):
        sib_copy(0 if n < 2 else 1, 4, n).wait_recv()
    add(place(0, 4), place(0, 4, sibling))

    rows_out = []
    for k in range(1, CLUS):
        e = (i + k) % CLUS
        c = pltpu.make_async_remote_copy(
            src_ref=total.at[pl.ds(e * OWN, OWN), :], dst_ref=landed.at[i],
            send_sem=row_send.at[k], recv_sem=row_recv.at[k],
            device_id=(s, e), device_id_type=MESH,
        )
        c.start()
        rows_out.append(c)
    landed[i] = total[pl.ds(i * OWN, OWN), :]
    for c in rows_out:
        c.wait_recv()
    for r in range(KC):
        row = landed[inv_s[r, 0]]
        for cb in range(OWN):
            out[pl.ds(r, 1), pl.ds(cb * BLK, BLK)] = row[cb : cb + 1]
    for c in rows_out:
        c.wait_send()
    for c in started:
        c.wait_send()


def body(duals, blocks, prob, cluster_map, block_cols, counts, cut_owner_rows):
    any_ = pl.BlockSpec(memory_space=pltpu.HBM)
    dma = pltpu.SemaphoreType.DMA
    return pl.pallas_call(
        kernel,
        out_shape=jax.ShapeDtypeStruct((KC, OWN * BLK), F32),
        in_specs=[any_] * 8,
        out_specs=pl.BlockSpec(memory_space=pltpu.VMEM),
        scratch_shapes=[
            pltpu.VMEM((ROWS, BLK, BLK), BF16),
            pltpu.VMEM((ROWS, BLK), BF16),
            pltpu.VMEM((1, 64), F32),
            pltpu.VMEM((1, 64), I32),
            pltpu.VMEM((2, 64), I32),
            pltpu.SMEM((1,), I32),
            pltpu.SMEM((256,), I32),
            pltpu.VMEM((1, 256), I32),
            pltpu.VMEM((16, 128), I32),
            pltpu.SMEM((16, 128), I32),
            pltpu.VMEM((SCEN, PIECE, BLK), F32),
            pltpu.VMEM((CLUS * OWN, BLK), F32),
            pltpu.VMEM((CLUS, OWN, BLK), F32),
            dma((8,)),
            dma((4,)),
            dma((2, 4, 4)),
            dma((2, 4, 4)),
            dma((2, 5, 4)),
            dma((2, 5, 4)),
            dma((CLUS,)),
            dma((CLUS,)),
        ],
        compiler_params=pltpu.CompilerParams(
            collective_id=0, has_side_effects=True, vmem_limit_bytes=63 << 20
        ),
    )(
        duals.reshape(ROWS, BLK),
        blocks.reshape(ROWS, BLK, BLK),
        prob.reshape(1, 64),
        cluster_map.reshape(1, 64),
        block_cols.T,
        counts,
        cut_owner_rows,
        cut_owner_rows.reshape(1, 256),
    )


def solution(mesh):
    placed = (
        P(("scen", "clus"), None, None),
        P(("scen", "clus"), None, None, None),
        P(("scen", "clus")),
        P(("scen", "clus")),
        P(("scen", "clus"), None),
        P(("scen", "clus")),
        P(),
    )
    return jax.shard_map(
        body, mesh=mesh, in_specs=placed, out_specs=P("clus", "scen"), check_vma=False
    )
```

time: 140 us -> 33.9 us (0.24)
  waiting for transfers between devices: 112 us -> 0 us
  Pallas kernels: 0 us -> 31.6 us
  between operations: 14.1 us -> 0.66 us
  matrix products: 8.91 us -> 0 us
  other arithmetic: 2.91 us -> 0 us
    reduce_scatter x1 -> x0, waiting for transfers between devices: 60.2 us -> none  [body(): lax.psum_scatter(summed.reshape(lax.axis_size('scen') * own_blocks, KC, w...]
    all_gather x1 -> x0, waiting for transfers between devices: 51.4 us -> none  [body(): lax.all_gather(reduced, 'clus', axis=0, tiled=True)]
    pallas_call x0 -> x1, Pallas kernels: none -> 31.6 us  [body(): pl.pallas_call(kernel, out_shape=jax.ShapeDtypeStruct((KC, OWN * BLK), F3...]
    dot_general x3 -> x0, matrix products: 8.91 us -> none  [the longest x1 3.37 us: body(): jnp.einsum('plqv,plq->plv', blocks, weighted_duals, preferred_element_typ...]
  transfers between devices with their start and end apart: 2 -> 0, of which waited for: 2 -> 0; matrix products, arithmetic and copies ran while one was open for 0% -> 0% of each run, Pallas kernels for 0% -> 0%
where the time goes in v1:
time: 33.9 us; the launch traced here: 33.8 us
  Pallas kernels  31.6 us (93%)
  local copies, waits for them, and re-layouts  1.57 us (5%)
  between operations  0.66 us (2%)
    pallas_call x1, Pallas kernels, body(): pl.pallas_call(kernel, out_shape=jax.ShapeDtypeStruct((KC, OWN * BLK), F3...  31.6 us
    unnamed x1, local copies, waits for them, and re-layouts  1.57 us

profile of v1, /device:TPU:1, one launch (start us, length us, event | category | flops | bytes accessed | tf_op | source)
XLA Modules:
  0.0 33.8 jit_solution(4555062992346232839)
XLA Ops:
  0.7 31.6 %shard_map.73 = f32[16,2048]{1,0:T(8,128)} custom-call(bf16[128,128]{1,0:T(8,128)(2,1)} %bitcast.7, bf16[128,128,128]{2,1,0:T(8,128)(2,1)} %bitcast.6, f32[1,64]{1,0:T(1,128)} %bitcast.10, s32[1,64]{1,0:T(1,128)} %bitcast.11, s32[2,64]{1,0:T(2,128)} %bitcast.9, s32[1]{0:T(128)S(6)} %copy.9.counts_h, s32[256]{0:T(256)} %owners_h.1, s32[1,256]{1,0:T(1,128)} %bitcast.8), custom_call_target="tpu_custom_call" | custom-call | tf_op jit(solution)/shard_map/pallas_call | solution.py:201
  32.3 1.6 %copy.10 = f32[16,2048]{1,0:T(8,128)} copy(f32[16,2048]{1,0:T(8,128)} %shard_map.73) | data formatting | bytes 262144

commit v2 on v1

--- a/solution.py
+++ b/solution.py
@@ -195,25 +195,213 @@
         c.wait_send()
 
 
+CAP = 23
+MSG = 24
+SLOT = 32
+RING = tuple((dz, dc) for dz in (4, 3, 5, 2, 6, 1, 7, 0) for dc in (0, 1) if (dz, dc) != (0, 0))
+TORUS = tuple(
+    sorted(
+        ((dy, dx) for dy in range(4) for dx in range(4) if (dy, dx) != (0, 0)),
+        key=lambda d: -(min(d[0], 4 - d[0]) + min(d[1], 4 - d[1])),
+    )
+)
+
+
+def routed(
+    duals_h, blocks_h, prob_h, cmap_h, cols_h, counts_h, owners_h, owners2_h, out, flag,
+    blk, dua, prb, cmp, col, cnt, own, ownv, inv_v, inv_s, prod, msgs, landed, total, rows,
+    small_sem, blk_sem, msg_send, msg_recv, row_send, row_recv,
+):
+    s, i = lax.axis_index("scen"), lax.axis_index("clus")
+    z, c, y, x = s // 2, s % 2, i // 4, i % 4
+    scen_peers = [(z + dz) % 8 * 2 + (c if dc == 0 else 1 - c) for dz, dc in RING]
+    clus_peers = [(y + dy) % 4 * 4 + (x + dx) % 4 for dy, dx in TORUS]
+
+    barrier = pltpu.get_barrier_semaphore()
+    for p in scen_peers:
+        pl.semaphore_signal(barrier, inc=1, device_id=(p, i), device_id_type=MESH)
+    for p in clus_peers:
+        pl.semaphore_signal(barrier, inc=1, device_id=(s, p), device_id_type=MESH)
+
+    smalls = [
+        pltpu.make_async_copy(src, dst, small_sem.at[n])
+        for n, (src, dst) in enumerate(
+            ((counts_h, cnt), (owners_h, own), (prob_h, prb), (duals_h, dua), (cmap_h, cmp), (cols_h, col), (owners2_h, ownv))
+        )
+    ]
+    for copy in smalls:
+        copy.start()
+    loads = []
+    for n in range(4):
+        part = pl.ds(32 * n, 32)
+        loads.append(pltpu.make_async_copy(blocks_h.at[part], blk.at[part], blk_sem.at[n]))
+        loads[-1].start()
+    for src in range(SCEN):
+        landed[src, pl.ds(MSG, SLOT - MSG), :] = jnp.zeros((SLOT - MSG, BLK), F32)
+    for copy in smalls:
+        copy.wait()
+
+    lane64 = lax.broadcasted_iota(I32, (1, 64), 1)
+    weight = jnp.where(lane64 < cnt[0], prb[...], 0.0)
+    spread = (lax.broadcasted_iota(I32, (ROWS, 64), 0) // 2) == lax.broadcasted_iota(I32, (ROWS, 64), 1)
+    weight_col = jnp.sum(jnp.where(spread, weight, 0.0), axis=1, keepdims=True)
+    weighted = (weight_col * dua[...].astype(F32)).astype(BF16).astype(F32)
+
+    pick = (
+        lax.broadcasted_iota(I32, (64, ROWS), 0) == lax.broadcasted_iota(I32, (64, ROWS), 1) // 2
+    ).astype(F32).astype(BF16)
+    both = jnp.dot(col[...].astype(F32).astype(BF16), pick, preferred_element_type=F32)
+    cluster = jnp.dot(cmp[...].astype(F32).astype(BF16), pick, preferred_element_type=F32).astype(I32)
+    lane = lax.broadcasted_iota(I32, (1, ROWS), 1)
+    column = jnp.where(lane % 2 == 0, both[0:1], both[1:2]).astype(I32)
+    live = lane // 2 < cnt[0]
+    dest = jnp.zeros((1, ROWS), I32)
+    for k in range(KC):
+        dest = jnp.where(cluster == k, own[i * KC + k] // KC, dest)
+    owner = jnp.where(live, column // OWN, -1)
+    target = dest * OWN + column % OWN + 1
+    mine = lax.broadcasted_iota(I32, (SCEN, ROWS), 0) == owner
+    before = (
+        lax.broadcasted_iota(I32, (ROWS, ROWS), 0) < lax.broadcasted_iota(I32, (ROWS, ROWS), 1)
+    ).astype(F32).astype(BF16)
+    ahead = jnp.dot(mine.astype(F32).astype(BF16), before, preferred_element_type=F32)
+    rank = jnp.sum(jnp.where(mine, ahead, 0.0), axis=0, keepdims=True).astype(I32)
+    over = jnp.max(rank, axis=1, keepdims=True) >= CAP
+    slot = jnp.where(live & (rank < CAP), owner * MSG + rank, -1)
+    gather = (lax.broadcasted_iota(I32, (SCEN * MSG, ROWS), 0) == slot).astype(F32).astype(BF16)
+    values = jnp.where(mine & (rank < CAP), target, 0).astype(F32).astype(BF16)
+    places = (
+        lax.broadcasted_iota(I32, (ROWS, ROWS), 0) == rank + s % 4 * SLOT
+    ).astype(F32).astype(BF16)
+    keys = lax.dot_general(values, places, (((1,), (1,)), ((), ())), preferred_element_type=F32)
+    keys = jnp.where(lax.broadcasted_iota(I32, (SCEN, ROWS), 1) == ROWS - 1, jnp.where(over, -1.0, 0.0), keys)
+
+    row16 = lax.broadcasted_iota(I32, (16, 256), 0)
+    lane256 = lax.broadcasted_iota(I32, (16, 256), 1)
+    inv_col = jnp.max(jnp.where(ownv[...] == i * KC + row16, lane256 // KC, 0), axis=1, keepdims=True)
+    inv_v[...] = jnp.broadcast_to(inv_col, (16, 128))
+    inverse = pltpu.make_async_copy(inv_v, inv_s, small_sem.at[7])
+    inverse.start()
+
+    sub = lax.broadcasted_iota(I32, (8, BLK), 0)
+    for t in range(ROWS // 8):
+        if t % 4 == 0:
+            loads[t // 4].wait()
+        w = weighted[8 * t : 8 * t + 8]
+        lhs = jnp.concatenate([jnp.where(sub == g, w, 0.0) for g in range(8)], axis=1).astype(BF16)
+        rhs = blk[8 * t : 8 * t + 8].reshape(8 * BLK, BLK)
+        prod[pl.ds(8 * t, 8), :] = jnp.dot(lhs, rhs, preferred_element_type=F32)
+
+    def exact(onehot, values):
+        high = values.astype(BF16)
+        low = (values - high.astype(F32)).astype(BF16)
+        return jnp.dot(onehot, high, preferred_element_type=F32) + jnp.dot(onehot, low, preferred_element_type=F32)
+
+    sent = exact(gather, prod[...])
+    for d in range(SCEN):
+        msgs[d] = sent[d * MSG : (d + 1) * MSG]
+    for d in range(SCEN):
+        msgs[d, pl.ds(CAP, 1), :] = keys[d : d + 1]
+
+    inverse.wait()
+    pl.semaphore_wait(barrier, len(RING) + len(TORUS))
+
+    def message(k, d, src):
+        return pltpu.make_async_remote_copy(
+            src_ref=msgs.at[d], dst_ref=landed.at[src, pl.ds(0, MSG), :],
+            send_sem=msg_send.at[k], recv_sem=msg_recv.at[src],
+            device_id=(d, i), device_id_type=MESH,
+        )
+
+    for k, p in enumerate(scen_peers):
+        message(k, p, s).start()
+    pltpu.make_async_copy(msgs.at[s], landed.at[s, pl.ds(0, MSG), :], msg_recv.at[s]).start()
+
+    cell = lax.broadcasted_iota(I32, (CLUS * OWN, ROWS), 0).astype(F32) + 1.0
+    least = jnp.zeros((1, ROWS), F32)
+    for n, step in enumerate((0, 1, 3, 2)):
+        group = (z // 2 + step) % 4 * 4
+        for a in range(4):
+            message(0, s, group + a).wait_recv()
+        key = landed[group, pl.ds(CAP, 1), :]
+        for a in range(1, 4):
+            key = key + landed[group + a, pl.ds(CAP, 1), :]
+        least = jnp.minimum(least, key)
+        part = exact((cell == key).astype(F32).astype(BF16), landed[pl.ds(group, 4)].reshape(4 * SLOT, BLK))
+        if n < 3:
+            total[...] = part if n == 0 else total[...] + part
+        else:
+            spoilt = jnp.where(jnp.min(least, axis=1, keepdims=True) < 0.0, jnp.float32(jnp.nan), 0.0)
+            total[...] = total[...] + (part + spoilt)
+
+    def row(k, e, src):
+        return pltpu.make_async_remote_copy(
+            src_ref=total.at[pl.ds(e * OWN, OWN), :], dst_ref=rows.at[src],
+            send_sem=row_send.at[k], recv_sem=row_recv.at[src],
+            device_id=(s, e), device_id_type=MESH,
+        )
+
+    for k, p in enumerate(clus_peers):
+        row(k, p, i).start()
+    pltpu.make_async_copy(total.at[pl.ds(i * OWN, OWN), :], rows.at[i], row_recv.at[i]).start()
+    for src in range(CLUS):
+        row(0, i, src).wait_recv()
+    seen = rows[0, pl.ds(0, 1), :]
+    for src in range(1, CLUS):
+        seen = seen + rows[src, pl.ds(0, 1), :]
+    bad = jnp.max(jnp.where(seen != seen, 1, 0))
+    flag[0, 0] = bad
+    for r in range(KC):
+        line = rows[inv_s[r, 0]]
+        for cb in range(OWN):
+            out[pl.ds(r, 1), pl.ds(cb * BLK, BLK)] = line[cb : cb + 1]
+    for k, p in enumerate(scen_peers):
+        message(k, p, s).wait_send()
+    for k, p in enumerate(clus_peers):
+        row(k, p, i).wait_send()
+
+
 def body(duals, blocks, prob, cluster_map, block_cols, counts, cut_owner_rows):
-    any_ = pl.BlockSpec(memory_space=pltpu.HBM)
     dma = pltpu.SemaphoreType.DMA
-    return pl.pallas_call(
-        kernel,
-        out_shape=jax.ShapeDtypeStruct((KC, OWN * BLK), F32),
-        in_specs=[any_] * 8,
-        out_specs=pl.BlockSpec(memory_space=pltpu.VMEM),
-        scratch_shapes=[
-            pltpu.VMEM((ROWS, BLK, BLK), BF16),
-            pltpu.VMEM((ROWS, BLK), BF16),
-            pltpu.VMEM((1, 64), F32),
-            pltpu.VMEM((1, 64), I32),
-            pltpu.VMEM((2, 64), I32),
-            pltpu.SMEM((1,), I32),
-            pltpu.SMEM((256,), I32),
-            pltpu.VMEM((1, 256), I32),
-            pltpu.VMEM((16, 128), I32),
-            pltpu.SMEM((16, 128), I32),
+    arrays = (
+        duals.reshape(ROWS, BLK),
+        blocks.reshape(ROWS, BLK, BLK),
+        prob.reshape(1, 64),
+        cluster_map.reshape(1, 64),
+        block_cols.T,
+        counts,
+        cut_owner_rows,
+        cut_owner_rows.reshape(1, 256),
+    )
+    inputs = [
+        pltpu.VMEM((ROWS, BLK, BLK), BF16),
+        pltpu.VMEM((ROWS, BLK), BF16),
+        pltpu.VMEM((1, 64), F32),
+        pltpu.VMEM((1, 64), I32),
+        pltpu.VMEM((2, 64), I32),
+        pltpu.SMEM((1,), I32),
+        pltpu.SMEM((256,), I32),
+        pltpu.VMEM((1, 256), I32),
+        pltpu.VMEM((16, 128), I32),
+        pltpu.SMEM((16, 128), I32),
+    ]
+    block = jax.ShapeDtypeStruct((KC, OWN * BLK), F32)
+    vmem = pl.BlockSpec(memory_space=pltpu.VMEM)
+
+    def call(fn, shapes, specs, scratch, cid):
+        return pl.pallas_call(
+            fn,
+            out_shape=shapes,
+            in_specs=[pl.BlockSpec(memory_space=pltpu.HBM)] * len(arrays),
+            out_specs=specs,
+            scratch_shapes=inputs + scratch,
+            compiler_params=pltpu.CompilerParams(
+                collective_id=cid, has_side_effects=True, vmem_limit_bytes=60 << 20
+            ),
+        )(*arrays)
+
+    def gathered():
+        scratch = [
             pltpu.VMEM((SCEN, PIECE, BLK), F32),
             pltpu.VMEM((CLUS * OWN, BLK), F32),
             pltpu.VMEM((CLUS, OWN, BLK), F32),
@@ -225,20 +413,25 @@
             dma((2, 5, 4)),
             dma((CLUS,)),
             dma((CLUS,)),
-        ],
-        compiler_params=pltpu.CompilerParams(
-            collective_id=0, has_side_effects=True, vmem_limit_bytes=63 << 20
-        ),
-    )(
-        duals.reshape(ROWS, BLK),
-        blocks.reshape(ROWS, BLK, BLK),
-        prob.reshape(1, 64),
-        cluster_map.reshape(1, 64),
-        block_cols.T,
-        counts,
-        cut_owner_rows,
-        cut_owner_rows.reshape(1, 256),
-    )
+        ]
+        return call(kernel, block, vmem, scratch, 0)
+
+    scratch = [
+        pltpu.VMEM((ROWS, BLK), F32),
+        pltpu.VMEM((SCEN, MSG, BLK), F32),
+        pltpu.VMEM((SCEN, SLOT, BLK), F32),
+        pltpu.VMEM((CLUS * OWN, BLK), F32),
+        pltpu.VMEM((CLUS, OWN, BLK), F32),
+        dma((8,)),
+        dma((4,)),
+        dma((SCEN,)),
+        dma((SCEN,)),
+        dma((CLUS,)),
+        dma((CLUS,)),
+    ]
+    flag = jax.ShapeDtypeStruct((1, 1), I32)
+    out, full = call(routed, (block, flag), (vmem, pl.BlockSpec(memory_space=pltpu.SMEM)), scratch, 1)
+    return lax.cond(full[0, 0] != 0, gathered, lambda: out)
 
 
 def solution(mesh):

time: 33.9 us -> 26.4 us (0.78)
  Pallas kernels: 31.6 us -> 24.2 us
  local copies, waits for them, and re-layouts: 1.57 us -> 0.68 us
  between operations: 0.66 us -> 1.33 us
    pallas_call x1, Pallas kernels: 31.6 us -> 24.2 us  [call(): pl.pallas_call(fn, out_shape=shapes, in_specs=[pl.BlockSpec(memory_space=...]
    unnamed x1 -> x11, local copies, waits for them, and re-layouts: 1.57 us -> 0.68 us
where the time goes in v2:
time: 26.4 us; the launch traced here: 26.2 us
  Pallas kernels  24.2 us (92%)
  between operations  1.33 us (5%)
  local copies, waits for them, and re-layouts  0.68 us (3%)
    pallas_call x1, Pallas kernels, call(): pl.pallas_call(fn, out_shape=shapes, in_specs=[pl.BlockSpec(memory_space=...  24.2 us
    unnamed x11, local copies, waits for them, and re-layouts  0.68 us

profile of v2, /device:TPU:1, one launch (start us, length us, event | category | flops | bytes accessed | tf_op | source)
XLA Modules:
  0.0 26.2 jit_solution(1810497138994463853)
XLA Ops:
  0.0 0.0 copy-start.1
  0.0 0.0 copy-start.2
  0.0 0.0 copy-start.4
  0.0 0.0 copy-start.3
  0.0 0.0 copy-start
  0.7 24.2 %shard_map.75 = (f32[16,2048]{1,0:T(8,128)S(1)}, s32[1,1]{1,0:T(1,128)}) custom-call(bf16[128,128]{1,0:T(8,128)(2,1)} %bitcast.9, bf16[128,128,128]{2,1,0:T(8,128)(2,1)} %bitcast.7, f32[1,64]{1,0:T(1,128)} %bitcast.16, s32[1,64]{1,0:T(1,128)} %bitcast.18, s32[2,64]{1,0:T(2,128)} %bitcast.14, s32[1]{0:T(128)S(6)} %copy.13.counts_h, s32[256]{0:T(256)} %owners_h.1, ...), custom_call_target="tpu_custom_call" | custom-call | tf_op jit(solution)/shard_map/pallas_call | solution.py:392
  25.5 0.0 copy-done.1
  25.5 0.0 copy-done.2
  25.5 0.0 copy-done.4
  25.5 0.0 copy-done.3
  25.6 0.0 copy-done
  25.6 0.7 %copy.14 = f32[16,2048]{1,0:T(8,128)} copy(f32[16,2048]{1,0:T(8,128)S(1)} %get-tuple-element.37) | data formatting | bytes 262144
  (1 shorter events, 0.0 us)
Async XLA Ops:
  0.0 25.5 %copy-start.1 = (s32[256]{0:T(256)S(1)}, s32[256]{0:T(256)}, u32[]{:S(2)}) copy-start(s32[256]{0:T(256)} %owners_h.1) | copy-start | bytes 3076
  0.0 25.5 %copy-start.2 = (s32[64,2]{0,1:T(2,128)S(1)}, s32[64,2]{0,1:T(2,128)}, u32[]{:S(2)}) copy-start(s32[64,2]{0,1:T(2,128)} %param.13) | copy-start | bytes 1540
  0.0 25.5 %copy-start.4 = (s32[64]{0:T(128)S(1)}, s32[64]{0:T(128)}, u32[]{:S(2)}) copy-start(s32[64]{0:T(128)} %param.12) | copy-start | bytes 772
  0.0 25.5 %copy-start.3 = (f32[64]{0:T(128)S(1)}, f32[64]{0:T(128)}, u32[]{:S(2)}) copy-start(f32[64]{0:T(128)} %param.11) | copy-start | bytes 772
  0.0 25.5 %copy-start = (bf16[64,2,128]{2,1,0:T(2,128)(2,1)S(1)}, bf16[64,2,128]{2,1,0:T(2,128)(2,1)}, u32[]{:S(2)}) copy-start(bf16[64,2,128]{2,1,0:T(2,128)(2,1)} %param.9) | copy-start | bytes 98308

commit v3 on v2

--- a/solution.py
+++ b/solution.py
@@ -57,7 +57,7 @@
         c.wait()
 
     lane64 = lax.broadcasted_iota(I32, (1, 64), 1)
-    weight = jnp.where(lane64 < cnt[0], prb[...], 0.0)
+    weight = jnp.where(lane64 < cnt[0, 0], prb[...], 0.0)
     spread = (lax.broadcasted_iota(I32, (ROWS, 64), 0) // 2) == lax.broadcasted_iota(I32, (ROWS, 64), 1)
     weight_col = jnp.sum(jnp.where(spread, weight, 0.0), axis=1, keepdims=True)
     weighted = (weight_col * dua[...].astype(F32)).astype(BF16).astype(F32)
@@ -220,8 +220,6 @@
     barrier = pltpu.get_barrier_semaphore()
     for p in scen_peers:
         pl.semaphore_signal(barrier, inc=1, device_id=(p, i), device_id_type=MESH)
-    for p in clus_peers:
-        pl.semaphore_signal(barrier, inc=1, device_id=(s, p), device_id_type=MESH)
 
     smalls = [
         pltpu.make_async_copy(src, dst, small_sem.at[n])
@@ -236,13 +234,17 @@
         part = pl.ds(32 * n, 32)
         loads.append(pltpu.make_async_copy(blocks_h.at[part], blk.at[part], blk_sem.at[n]))
         loads[-1].start()
+
+    for p in clus_peers:
+        pl.semaphore_signal(barrier, inc=1, device_id=(s, p), device_id_type=MESH)
+
     for src in range(SCEN):
         landed[src, pl.ds(MSG, SLOT - MSG), :] = jnp.zeros((SLOT - MSG, BLK), F32)
     for copy in smalls:
         copy.wait()
 
     lane64 = lax.broadcasted_iota(I32, (1, 64), 1)
-    weight = jnp.where(lane64 < cnt[0], prb[...], 0.0)
+    weight = jnp.where(lane64 < cnt[0, 0], prb[...], 0.0)
     spread = (lax.broadcasted_iota(I32, (ROWS, 64), 0) // 2) == lax.broadcasted_iota(I32, (ROWS, 64), 1)
     weight_col = jnp.sum(jnp.where(spread, weight, 0.0), axis=1, keepdims=True)
     weighted = (weight_col * dua[...].astype(F32)).astype(BF16).astype(F32)
@@ -254,7 +256,7 @@
     cluster = jnp.dot(cmp[...].astype(F32).astype(BF16), pick, preferred_element_type=F32).astype(I32)
     lane = lax.broadcasted_iota(I32, (1, ROWS), 1)
     column = jnp.where(lane % 2 == 0, both[0:1], both[1:2]).astype(I32)
-    live = lane // 2 < cnt[0]
+    live = lane // 2 < cnt[0, 0]
     dest = jnp.zeros((1, ROWS), I32)
     for k in range(KC):
         dest = jnp.where(cluster == k, own[i * KC + k] // KC, dest)
@@ -369,7 +371,7 @@
         prob.reshape(1, 64),
         cluster_map.reshape(1, 64),
         block_cols.T,
-        counts,
+        counts.reshape(1, 1),
         cut_owner_rows,
         cut_owner_rows.reshape(1, 256),
     )
@@ -379,13 +381,13 @@
         pltpu.VMEM((1, 64), F32),
         pltpu.VMEM((1, 64), I32),
         pltpu.VMEM((2, 64), I32),
-        pltpu.SMEM((1,), I32),
+        pltpu.SMEM((1, 1), I32),
         pltpu.SMEM((256,), I32),
         pltpu.VMEM((1, 256), I32),
         pltpu.VMEM((16, 128), I32),
         pltpu.SMEM((16, 128), I32),
     ]
-    block = jax.ShapeDtypeStruct((KC, OWN * BLK), F32)
+    block = pltpu.VMEM((KC, OWN * BLK), F32)
     vmem = pl.BlockSpec(memory_space=pltpu.VMEM)
 
     def call(fn, shapes, specs, scratch, cid):
@@ -429,9 +431,9 @@
         dma((CLUS,)),
         dma((CLUS,)),
     ]
-    flag = jax.ShapeDtypeStruct((1, 1), I32)
+    flag = pltpu.SMEM((1, 1), I32)
     out, full = call(routed, (block, flag), (vmem, pl.BlockSpec(memory_space=pltpu.SMEM)), scratch, 1)
-    return lax.cond(full[0, 0] != 0, gathered, lambda: out)
+    return lax.switch(full[0, 0], (lambda: out, gathered))
 
 
 def solution(mesh):

time: 26.4 us -> 24.7 us (0.936)
  Pallas kernels: 24.2 us -> 23.1 us
  between operations: 1.33 us -> 0.78 us
    pallas_call x1, Pallas kernels: 24.2 us -> 23.1 us  [call(): pl.pallas_call(fn, out_shape=shapes, in_specs=[pl.BlockSpec(memory_space=...]
where the time goes in v3:
time: 24.7 us; the launch traced here: 24.6 us
  Pallas kernels  23.1 us (94%)
  between operations  0.78 us (3%)
  local copies, waits for them, and re-layouts  0.68 us (3%)
    pallas_call x1, Pallas kernels, call(): pl.pallas_call(fn, out_shape=shapes, in_specs=[pl.BlockSpec(memory_space=...  23.1 us
    unnamed x11, local copies, waits for them, and re-layouts  0.68 us

profile of v3, /device:TPU:1, one launch (start us, length us, event | category | flops | bytes accessed | tf_op | source)
XLA Modules:
  0.0 24.6 jit_solution(9364773233141952337)
XLA Ops:
  0.0 0.0 copy-start.1
  0.0 0.0 copy-start.2
  0.0 0.0 copy-start.4
  0.0 0.0 copy-start.3
  0.0 0.0 copy-start
  0.7 23.1 %shard_map.75 = (f32[16,2048]{1,0:T(8,128)S(1)}, s32[1,1]{1,0:T(1,128)S(4)}) custom-call(bf16[128,128]{1,0:T(8,128)(2,1)} %bitcast.11, bf16[128,128,128]{2,1,0:T(8,128)(2,1)} %bitcast.9, f32[1,64]{1,0:T(1,128)} %bitcast.18, s32[1,64]{1,0:T(1,128)} %bitcast.20, s32[2,64]{1,0:T(2,128)} %bitcast.16, s32[1,1]{1,0:T(1,128)} %bitcast.8.counts_h, s32[256]{0:T(256)} %owners_h.1, ...), custom_call_target="tpu_custom_call" | custom-call | tf_op jit(solution)/shard_map/pallas_call | solution.py:394
  23.9 0.0 copy-done.1
  23.9 0.0 copy-done.2
  23.9 0.0 copy-done.4
  23.9 0.0 copy-done.3
  23.9 0.0 copy-done
  23.9 0.7 %copy.13 = f32[16,2048]{1,0:T(8,128)} copy(f32[16,2048]{1,0:T(8,128)S(1)} %get-tuple-element.37) | data formatting | bytes 262144
  (1 shorter events, 0.0 us)
Async XLA Ops:
  0.0 23.9 %copy-start.1 = (s32[256]{0:T(256)S(1)}, s32[256]{0:T(256)}, u32[]{:S(2)}) copy-start(s32[256]{0:T(256)} %owners_h.1) | copy-start | bytes 3076
  0.0 23.9 %copy-start.2 = (s32[64,2]{0,1:T(2,128)S(1)}, s32[64,2]{0,1:T(2,128)}, u32[]{:S(2)}) copy-start(s32[64,2]{0,1:T(2,128)} %param.13) | copy-start | bytes 1540
  0.0 23.9 %copy-start.4 = (s32[64]{0:T(128)S(1)}, s32[64]{0:T(128)}, u32[]{:S(2)}) copy-start(s32[64]{0:T(128)} %param.12) | copy-start | bytes 772
  0.0 23.9 %copy-start.3 = (f32[64]{0:T(128)S(1)}, f32[64]{0:T(128)}, u32[]{:S(2)}) copy-start(f32[64]{0:T(128)} %param.11) | copy-start | bytes 772
  0.0 23.9 %copy-start = (bf16[64,2,128]{2,1,0:T(2,128)(2,1)S(1)}, bf16[64,2,128]{2,1,0:T(2,128)(2,1)}, u32[]{:S(2)}) copy-start(bf16[64,2,128]{2,1,0:T(2,128)(2,1)} %param.9) | copy-start | bytes 98308

commit v4 on v3

--- a/solution.py
+++ b/solution.py
@@ -195,9 +195,10 @@
         c.wait_send()
 
 
-CAP = 23
-MSG = 24
-SLOT = 32
+CAP = 15
+MSG = 16
+SPARE = 7
+PACK = 8
 RING = tuple((dz, dc) for dz in (4, 3, 5, 2, 6, 1, 7, 0) for dc in (0, 1) if (dz, dc) != (0, 0))
 TORUS = tuple(
     sorted(
@@ -210,17 +211,14 @@
 def routed(
     duals_h, blocks_h, prob_h, cmap_h, cols_h, counts_h, owners_h, owners2_h, out, flag,
     blk, dua, prb, cmp, col, cnt, own, ownv, inv_v, inv_s, prod, msgs, landed, total, rows,
-    small_sem, blk_sem, msg_send, msg_recv, row_send, row_recv,
+    pack1, pack2, spare1, spare2, late,
+    small_sem, blk_sem, msg_send, msg_recv, row_send, row_recv, first_send, first_recv, second_send, second_recv,
 ):
     s, i = lax.axis_index("scen"), lax.axis_index("clus")
     z, c, y, x = s // 2, s % 2, i // 4, i % 4
     scen_peers = [(z + dz) % 8 * 2 + (c if dc == 0 else 1 - c) for dz, dc in RING]
     clus_peers = [(y + dy) % 4 * 4 + (x + dx) % 4 for dy, dx in TORUS]
 
-    barrier = pltpu.get_barrier_semaphore()
-    for p in scen_peers:
-        pl.semaphore_signal(barrier, inc=1, device_id=(p, i), device_id_type=MESH)
-
     smalls = [
         pltpu.make_async_copy(src, dst, small_sem.at[n])
         for n, (src, dst) in enumerate(
@@ -230,16 +228,19 @@
     for copy in smalls:
         copy.start()
     loads = []
-    for n in range(4):
-        part = pl.ds(32 * n, 32)
+    for n, (at, many) in enumerate(((0, 64), (64, 64))):
+        part = pl.ds(at, many)
         loads.append(pltpu.make_async_copy(blocks_h.at[part], blk.at[part], blk_sem.at[n]))
         loads[-1].start()
 
+
+    barrier = pltpu.get_barrier_semaphore()
+    for p in scen_peers:
+        pl.semaphore_signal(barrier, inc=1, device_id=(p, i), device_id_type=MESH)
+
     for p in clus_peers:
         pl.semaphore_signal(barrier, inc=1, device_id=(s, p), device_id_type=MESH)
 
-    for src in range(SCEN):
-        landed[src, pl.ds(MSG, SLOT - MSG), :] = jnp.zeros((SLOT - MSG, BLK), F32)
     for copy in smalls:
         copy.wait()
 
@@ -249,9 +250,10 @@
     weight_col = jnp.sum(jnp.where(spread, weight, 0.0), axis=1, keepdims=True)
     weighted = (weight_col * dua[...].astype(F32)).astype(BF16).astype(F32)
 
-    pick = (
-        lax.broadcasted_iota(I32, (64, ROWS), 0) == lax.broadcasted_iota(I32, (64, ROWS), 1) // 2
-    ).astype(F32).astype(BF16)
+    def as_bf16(mask):
+        return mask.astype(F32).astype(BF16)
+
+    pick = as_bf16(lax.broadcasted_iota(I32, (64, ROWS), 0) == lax.broadcasted_iota(I32, (64, ROWS), 1) // 2)
     both = jnp.dot(col[...].astype(F32).astype(BF16), pick, preferred_element_type=F32)
     cluster = jnp.dot(cmp[...].astype(F32).astype(BF16), pick, preferred_element_type=F32).astype(I32)
     lane = lax.broadcasted_iota(I32, (1, ROWS), 1)
@@ -261,22 +263,33 @@
     for k in range(KC):
         dest = jnp.where(cluster == k, own[i * KC + k] // KC, dest)
     owner = jnp.where(live, column // OWN, -1)
-    target = dest * OWN + column % OWN + 1
+    target = dest * OWN + column % OWN
     mine = lax.broadcasted_iota(I32, (SCEN, ROWS), 0) == owner
-    before = (
-        lax.broadcasted_iota(I32, (ROWS, ROWS), 0) < lax.broadcasted_iota(I32, (ROWS, ROWS), 1)
-    ).astype(F32).astype(BF16)
-    ahead = jnp.dot(mine.astype(F32).astype(BF16), before, preferred_element_type=F32)
+    sublane = lax.broadcasted_iota(I32, (ROWS, ROWS), 0)
+    before = as_bf16(sublane < lax.broadcasted_iota(I32, (ROWS, ROWS), 1))
+    ahead = jnp.dot(as_bf16(mine), before, preferred_element_type=F32)
     rank = jnp.sum(jnp.where(mine, ahead, 0.0), axis=0, keepdims=True).astype(I32)
-    over = jnp.max(rank, axis=1, keepdims=True) >= CAP
-    slot = jnp.where(live & (rank < CAP), owner * MSG + rank, -1)
-    gather = (lax.broadcasted_iota(I32, (SCEN * MSG, ROWS), 0) == slot).astype(F32).astype(BF16)
-    values = jnp.where(mine & (rank < CAP), target, 0).astype(F32).astype(BF16)
-    places = (
-        lax.broadcasted_iota(I32, (ROWS, ROWS), 0) == rank + s % 4 * SLOT
-    ).astype(F32).astype(BF16)
-    keys = lax.dot_general(values, places, (((1,), (1,)), ((), ())), preferred_element_type=F32)
-    keys = jnp.where(lax.broadcasted_iota(I32, (SCEN, ROWS), 1) == ROWS - 1, jnp.where(over, -1.0, 0.0), keys)
+    fits = live & (rank < CAP)
+    spare = live & (rank >= CAP)
+    spare_rank = jnp.dot(as_bf16(spare), before, preferred_element_type=F32).astype(I32)
+    packed = spare & (spare_rank < SPARE)
+    over = jnp.max(jnp.where(spare, spare_rank, 0), axis=1, keepdims=True) >= SPARE
+    slot = jnp.where(fits, owner * MSG + rank, jnp.where(packed, SCEN * MSG + spare_rank, -1))
+    gather = as_bf16(lax.broadcasted_iota(I32, (SCEN * MSG + PACK, ROWS), 0) == slot)
+
+    def along_lanes(values, places):
+        return lax.dot_general(
+            values.astype(F32).astype(BF16), as_bf16(sublane == places), (((1,), (1,)), ((), ())), preferred_element_type=F32
+        )
+
+    keys = along_lanes(jnp.where(mine & fits, target + 1, 0), rank + s % 8 * MSG)
+
+    def pack_keys(taken, device, place, lanes, spoilt, number):
+        one = along_lanes(jnp.where(taken, device + 1, 0), lanes)
+        two = along_lanes(jnp.where(taken, place, 0), lanes)
+        return jnp.where(lane == number * PACK + SPARE, jnp.where(spoilt, -1.0, 0.0), one * 256.0 + two)
+
+    spare_keys = pack_keys(packed, owner, target, spare_rank + i * PACK, over, i)
 
     row16 = lax.broadcasted_iota(I32, (16, 256), 0)
     lane256 = lax.broadcasted_iota(I32, (16, 256), 1)
@@ -287,8 +300,8 @@
 
     sub = lax.broadcasted_iota(I32, (8, BLK), 0)
     for t in range(ROWS // 8):
-        if t % 4 == 0:
-            loads[t // 4].wait()
+        if t in {0: 0, 8: 1}:
+            loads[{0: 0, 8: 1}[t]].wait()
         w = weighted[8 * t : 8 * t + 8]
         lhs = jnp.concatenate([jnp.where(sub == g, w, 0.0) for g in range(8)], axis=1).astype(BF16)
         rhs = blk[8 * t : 8 * t + 8].reshape(8 * BLK, BLK)
@@ -300,41 +313,74 @@
         return jnp.dot(onehot, high, preferred_element_type=F32) + jnp.dot(onehot, low, preferred_element_type=F32)
 
     sent = exact(gather, prod[...])
+    last = lax.broadcasted_iota(I32, (MSG, BLK), 0) == CAP
     for d in range(SCEN):
-        msgs[d] = sent[d * MSG : (d + 1) * MSG]
-    for d in range(SCEN):
-        msgs[d, pl.ds(CAP, 1), :] = keys[d : d + 1]
+        msgs[d] = jnp.where(last, keys[d : d + 1], sent[d * MSG : (d + 1) * MSG])
+    pack1[...] = jnp.where(sub == SPARE, spare_keys, sent[SCEN * MSG :])
 
     inverse.wait()
     pl.semaphore_wait(barrier, len(RING) + len(TORUS))
 
     def message(k, d, src):
         return pltpu.make_async_remote_copy(
-            src_ref=msgs.at[d], dst_ref=landed.at[src, pl.ds(0, MSG), :],
+            src_ref=msgs.at[d], dst_ref=landed.at[src],
             send_sem=msg_send.at[k], recv_sem=msg_recv.at[src],
             device_id=(d, i), device_id_type=MESH,
         )
 
+    def first(k, e, src):
+        return pltpu.make_async_remote_copy(
+            src_ref=pack1, dst_ref=spare1.at[src], send_sem=first_send.at[k], recv_sem=first_recv.at[src],
+            device_id=(s, e), device_id_type=MESH,
+        )
+
+    def second(k, d, src):
+        return pltpu.make_async_remote_copy(
+            src_ref=pack2, dst_ref=spare2.at[src], send_sem=second_send.at[k], recv_sem=second_recv.at[src],
+            device_id=(d, i), device_id_type=MESH,
+        )
+
+    for k in range(15):
+        message(k, scen_peers[k], s).start()
+        first(k, clus_peers[k], i).start()
+    pltpu.make_async_copy(msgs.at[s], landed.at[s], msg_recv.at[s]).start()
+    pltpu.make_async_copy(pack1, spare1.at[i], first_recv.at[i]).start()
+
+    def read_keys(spares):
+        key = spares[0, pl.ds(SPARE, 1), :]
+        for n in range(1, 16):
+            key = key + spares[n, pl.ds(SPARE, 1), :]
+        whole = key.astype(I32)
+        return key > 0.0, whole // 256 - 1, whole % 256, jnp.min(key, axis=1, keepdims=True) < 0.0
+
+    for src in range(CLUS):
+        first(0, i, src).wait_recv()
+    valid, device, place, spoilt = read_keys(spare1)
+    cut = place // OWN
+    counted = jnp.sum(
+        jnp.where(valid & (lax.broadcasted_iota(I32, (CLUS, ROWS), 0) == cut), 1.0, 0.0), axis=1, keepdims=True
+    )
+    spoilt = spoilt | (jnp.max(counted, axis=0, keepdims=True) > SPARE)
+    hit = valid & (cut == i)
+    hit_rank = jnp.dot(as_bf16(hit), before, preferred_element_type=F32).astype(I32)
+    hit = hit & (hit_rank < SPARE)
+    second_keys = pack_keys(hit, device, lane // PACK * OWN + place % OWN, hit_rank + s * PACK, spoilt, s)
+    moved = exact(as_bf16((sub == hit_rank) & hit), spare1[...].reshape(ROWS, BLK))
+    pack2[...] = jnp.where(sub == SPARE, second_keys, moved)
     for k, p in enumerate(scen_peers):
-        message(k, p, s).start()
-    pltpu.make_async_copy(msgs.at[s], landed.at[s, pl.ds(0, MSG), :], msg_recv.at[s]).start()
-
-    cell = lax.broadcasted_iota(I32, (CLUS * OWN, ROWS), 0).astype(F32) + 1.0
-    least = jnp.zeros((1, ROWS), F32)
-    for n, step in enumerate((0, 1, 3, 2)):
-        group = (z // 2 + step) % 4 * 4
-        for a in range(4):
+        second(k, p, s).start()
+    pltpu.make_async_copy(pack2, spare2.at[s], second_recv.at[s]).start()
+
+    cell = lax.broadcasted_iota(I32, (CLUS * OWN, ROWS), 0)
+    for step in range(2):
+        group = (z // 4 + step) % 2 * 8
+        for a in range(8):
             message(0, s, group + a).wait_recv()
         key = landed[group, pl.ds(CAP, 1), :]
-        for a in range(1, 4):
+        for a in range(1, 8):
             key = key + landed[group + a, pl.ds(CAP, 1), :]
-        least = jnp.minimum(least, key)
-        part = exact((cell == key).astype(F32).astype(BF16), landed[pl.ds(group, 4)].reshape(4 * SLOT, BLK))
-        if n < 3:
-            total[...] = part if n == 0 else total[...] + part
-        else:
-            spoilt = jnp.where(jnp.min(least, axis=1, keepdims=True) < 0.0, jnp.float32(jnp.nan), 0.0)
-            total[...] = total[...] + (part + spoilt)
+        part = exact(as_bf16(cell == key.astype(I32) - 1), landed[pl.ds(group, 8)].reshape(8 * MSG, BLK))
+        total[...] = part if step == 0 else total[...] + part
 
     def row(k, e, src):
         return pltpu.make_async_remote_copy(
@@ -348,19 +394,21 @@
     pltpu.make_async_copy(total.at[pl.ds(i * OWN, OWN), :], rows.at[i], row_recv.at[i]).start()
     for src in range(CLUS):
         row(0, i, src).wait_recv()
-    seen = rows[0, pl.ds(0, 1), :]
-    for src in range(1, CLUS):
-        seen = seen + rows[src, pl.ds(0, 1), :]
-    bad = jnp.max(jnp.where(seen != seen, 1, 0))
-    flag[0, 0] = bad
+    for src in range(SCEN):
+        second(0, s, src).wait_recv()
+    valid, device, place, spoilt = read_keys(spare2)
+    here = as_bf16(cell == jnp.where(valid & (device == s), place, -1))
+    late[...] = exact(here, spare2[...].reshape(ROWS, BLK)).reshape(CLUS, OWN, BLK)
+    flag[0, 0] = jnp.max(jnp.where(spoilt, 1, 0))
     for r in range(KC):
-        line = rows[inv_s[r, 0]]
+        line = rows[inv_s[r, 0]] + late[inv_s[r, 0]]
         for cb in range(OWN):
             out[pl.ds(r, 1), pl.ds(cb * BLK, BLK)] = line[cb : cb + 1]
-    for k, p in enumerate(scen_peers):
-        message(k, p, s).wait_send()
-    for k, p in enumerate(clus_peers):
-        row(k, p, i).wait_send()
+    for k in range(15):
+        message(k, scen_peers[k], s).wait_send()
+        second(k, scen_peers[k], s).wait_send()
+        first(k, clus_peers[k], i).wait_send()
+        row(k, clus_peers[k], i).wait_send()
 
 
 def body(duals, blocks, prob, cluster_map, block_cols, counts, cut_owner_rows):
@@ -421,16 +469,17 @@
     scratch = [
         pltpu.VMEM((ROWS, BLK), F32),
         pltpu.VMEM((SCEN, MSG, BLK), F32),
-        pltpu.VMEM((SCEN, SLOT, BLK), F32),
+        pltpu.VMEM((SCEN, MSG, BLK), F32),
         pltpu.VMEM((CLUS * OWN, BLK), F32),
+        pltpu.VMEM((CLUS, OWN, BLK), F32),
+        pltpu.VMEM((PACK, BLK), F32),
+        pltpu.VMEM((PACK, BLK), F32),
+        pltpu.VMEM((CLUS, PACK, BLK), F32),
+        pltpu.VMEM((SCEN, PACK, BLK), F32),
         pltpu.VMEM((CLUS, OWN, BLK), F32),
         dma((8,)),
         dma((4,)),
-        dma((SCEN,)),
-        dma((SCEN,)),
-        dma((CLUS,)),
-        dma((CLUS,)),
-    ]
+    ] + [dma((16,))] * 8
     flag = pltpu.SMEM((1, 1), I32)
     out, full = call(routed, (block, flag), (vmem, pl.BlockSpec(memory_space=pltpu.SMEM)), scratch, 1)
     return lax.switch(full[0, 0], (lambda: out, gathered))

time: 24.7 us -> 24 us (0.972)
  Pallas kernels: 23.1 us -> 22.4 us
    pallas_call x1, Pallas kernels: 23.1 us -> 22.4 us  [call(): pl.pallas_call(fn, out_shape=shapes, in_specs=[pl.BlockSpec(memory_space=...]
where the time goes in v4:
time: 24 us; the launch traced here: 23.8 us
  Pallas kernels  22.4 us (93%)
  between operations  0.78 us (3%)
  local copies, waits for them, and re-layouts  0.68 us (3%)
    pallas_call x1, Pallas kernels, call(): pl.pallas_call(fn, out_shape=shapes, in_specs=[pl.BlockSpec(memory_space=...  22.4 us
    unnamed x11, local copies, waits for them, and re-layouts  0.68 us

profile of v4, /device:TPU:1, one launch (start us, length us, event | category | flops | bytes accessed | tf_op | source)
XLA Modules:
  0.0 23.8 jit_solution(6515153912587225988)
XLA Ops:
  0.0 0.0 copy-start.1
  0.0 0.0 copy-start.2
  0.0 0.0 copy-start.4
  0.0 0.0 copy-start.3
  0.0 0.0 copy-start
  0.7 22.4 %shard_map.75 = (f32[16,2048]{1,0:T(8,128)S(1)}, s32[1,1]{1,0:T(1,128)S(4)}) custom-call(bf16[128,128]{1,0:T(8,128)(2,1)} %bitcast.11, bf16[128,128,128]{2,1,0:T(8,128)(2,1)} %bitcast.9, f32[1,64]{1,0:T(1,128)} %bitcast.18, s32[1,64]{1,0:T(1,128)} %bitcast.20, s32[2,64]{1,0:T(2,128)} %bitcast.16, s32[1,1]{1,0:T(1,128)} %bitcast.8.counts_h, s32[256]{0:T(256)} %owners_h.1, ...), custom_call_target="tpu_custom_call" | custom-call | tf_op jit(solution)/shard_map/pallas_call | solution.py:442
  23.1 0.0 copy-done.1
  23.1 0.0 copy-done.2
  23.1 0.0 copy-done.4
  23.2 0.0 copy-done.3
  23.2 0.0 copy-done
  23.2 0.7 %copy.13 = f32[16,2048]{1,0:T(8,128)} copy(f32[16,2048]{1,0:T(8,128)S(1)} %get-tuple-element.37) | data formatting | bytes 262144
  (1 shorter events, 0.0 us)
Async XLA Ops:
  0.0 23.1 %copy-start.1 = (s32[256]{0:T(256)S(1)}, s32[256]{0:T(256)}, u32[]{:S(2)}) copy-start(s32[256]{0:T(256)} %owners_h.1) | copy-start | bytes 3076
  0.0 23.1 %copy-start.2 = (s32[64,2]{0,1:T(2,128)S(1)}, s32[64,2]{0,1:T(2,128)}, u32[]{:S(2)}) copy-start(s32[64,2]{0,1:T(2,128)} %param.13) | copy-start | bytes 1540
  0.0 23.1 %copy-start.4 = (s32[64]{0:T(128)S(1)}, s32[64]{0:T(128)}, u32[]{:S(2)}) copy-start(s32[64]{0:T(128)} %param.12) | copy-start | bytes 772
  0.0 23.1 %copy-start.3 = (f32[64]{0:T(128)S(1)}, f32[64]{0:T(128)}, u32[]{:S(2)}) copy-start(f32[64]{0:T(128)} %param.11) | copy-start | bytes 772
  0.0 23.1 %copy-start = (bf16[64,2,128]{2,1,0:T(2,128)(2,1)S(1)}, bf16[64,2,128]{2,1,0:T(2,128)(2,1)}, u32[]{:S(2)}) copy-start(bf16[64,2,128]{2,1,0:T(2,128)(2,1)} %param.9) | copy-start | bytes 98308

commit v5 on v4

--- a/solution.py
+++ b/solution.py
@@ -291,13 +291,6 @@
 
     spare_keys = pack_keys(packed, owner, target, spare_rank + i * PACK, over, i)
 
-    row16 = lax.broadcasted_iota(I32, (16, 256), 0)
-    lane256 = lax.broadcasted_iota(I32, (16, 256), 1)
-    inv_col = jnp.max(jnp.where(ownv[...] == i * KC + row16, lane256 // KC, 0), axis=1, keepdims=True)
-    inv_v[...] = jnp.broadcast_to(inv_col, (16, 128))
-    inverse = pltpu.make_async_copy(inv_v, inv_s, small_sem.at[7])
-    inverse.start()
-
     sub = lax.broadcasted_iota(I32, (8, BLK), 0)
     for t in range(ROWS // 8):
         if t in {0: 0, 8: 1}:
@@ -318,7 +311,6 @@
         msgs[d] = jnp.where(last, keys[d : d + 1], sent[d * MSG : (d + 1) * MSG])
     pack1[...] = jnp.where(sub == SPARE, spare_keys, sent[SCEN * MSG :])
 
-    inverse.wait()
     pl.semaphore_wait(barrier, len(RING) + len(TORUS))
 
     def message(k, d, src):
@@ -341,10 +333,18 @@
         )
 
     for k in range(15):
+        first(k, clus_peers[k], i).start()
+    for k in range(15):
         message(k, scen_peers[k], s).start()
-        first(k, clus_peers[k], i).start()
     pltpu.make_async_copy(msgs.at[s], landed.at[s], msg_recv.at[s]).start()
     pltpu.make_async_copy(pack1, spare1.at[i], first_recv.at[i]).start()
+
+    row16 = lax.broadcasted_iota(I32, (16, 256), 0)
+    lane256 = lax.broadcasted_iota(I32, (16, 256), 1)
+    inv_col = jnp.max(jnp.where(ownv[...] == i * KC + row16, lane256 // KC, 0), axis=1, keepdims=True)
+    inv_v[...] = jnp.broadcast_to(inv_col, (16, 128))
+    inverse = pltpu.make_async_copy(inv_v, inv_s, small_sem.at[7])
+    inverse.start()
 
     def read_keys(spares):
         key = spares[0, pl.ds(SPARE, 1), :]
@@ -392,14 +392,15 @@
     for k, p in enumerate(clus_peers):
         row(k, p, i).start()
     pltpu.make_async_copy(total.at[pl.ds(i * OWN, OWN), :], rows.at[i], row_recv.at[i]).start()
-    for src in range(CLUS):
-        row(0, i, src).wait_recv()
+    inverse.wait()
     for src in range(SCEN):
         second(0, s, src).wait_recv()
     valid, device, place, spoilt = read_keys(spare2)
     here = as_bf16(cell == jnp.where(valid & (device == s), place, -1))
     late[...] = exact(here, spare2[...].reshape(ROWS, BLK)).reshape(CLUS, OWN, BLK)
     flag[0, 0] = jnp.max(jnp.where(spoilt, 1, 0))
+    for src in range(CLUS):
+        row(0, i, src).wait_recv()
     for r in range(KC):
         line = rows[inv_s[r, 0]] + late[inv_s[r, 0]]
         for cb in range(OWN):

time: 24 us -> 23.9 us (level)
  no operation moved by 1% of the time
where the time goes in v5:
time: 23.9 us; the launch traced here: 23.8 us
  Pallas kernels  22.3 us (93%)
  between operations  0.78 us (3%)
  local copies, waits for them, and re-layouts  0.68 us (3%)
    pallas_call x1, Pallas kernels, call(): pl.pallas_call(fn, out_shape=shapes, in_specs=[pl.BlockSpec(memory_space=...  22.3 us
    unnamed x11, local copies, waits for them, and re-layouts  0.68 us

profile of v5, /device:TPU:1, one launch (start us, length us, event | category | flops | bytes accessed | tf_op | source)
XLA Modules:
  0.0 23.8 jit_solution(1264733824387769783)
XLA Ops:
  0.0 0.0 copy-start.1
  0.0 0.0 copy-start.2
  0.0 0.0 copy-start.4
  0.0 0.0 copy-start.3
  0.0 0.0 copy-start
  0.7 22.3 %shard_map.75 = (f32[16,2048]{1,0:T(8,128)S(1)}, s32[1,1]{1,0:T(1,128)S(4)}) custom-call(bf16[128,128]{1,0:T(8,128)(2,1)} %bitcast.11, bf16[128,128,128]{2,1,0:T(8,128)(2,1)} %bitcast.9, f32[1,64]{1,0:T(1,128)} %bitcast.18, s32[1,64]{1,0:T(1,128)} %bitcast.20, s32[2,64]{1,0:T(2,128)} %bitcast.16, s32[1,1]{1,0:T(1,128)} %bitcast.8.counts_h, s32[256]{0:T(256)} %owners_h.1, ...), custom_call_target="tpu_custom_call" | custom-call | tf_op jit(solution)/shard_map/pallas_call | solution.py:443
  23.1 0.0 copy-done.1
  23.1 0.0 copy-done.2
  23.1 0.0 copy-done.4
  23.1 0.0 copy-done.3
  23.1 0.0 copy-done
  23.1 0.7 %copy.13 = f32[16,2048]{1,0:T(8,128)} copy(f32[16,2048]{1,0:T(8,128)S(1)} %get-tuple-element.37) | data formatting | bytes 262144
  (1 shorter events, 0.0 us)
Async XLA Ops:
  0.0 23.1 %copy-start.1 = (s32[256]{0:T(256)S(1)}, s32[256]{0:T(256)}, u32[]{:S(2)}) copy-start(s32[256]{0:T(256)} %owners_h.1) | copy-start | bytes 3076
  0.0 23.1 %copy-start.2 = (s32[64,2]{0,1:T(2,128)S(1)}, s32[64,2]{0,1:T(2,128)}, u32[]{:S(2)}) copy-start(s32[64,2]{0,1:T(2,128)} %param.13) | copy-start | bytes 1540
  0.0 23.1 %copy-start.4 = (s32[64]{0:T(128)S(1)}, s32[64]{0:T(128)}, u32[]{:S(2)}) copy-start(s32[64]{0:T(128)} %param.12) | copy-start | bytes 772
  0.0 23.1 %copy-start.3 = (f32[64]{0:T(128)S(1)}, f32[64]{0:T(128)}, u32[]{:S(2)}) copy-start(f32[64]{0:T(128)} %param.11) | copy-start | bytes 772
  0.0 23.1 %copy-start = (bf16[64,2,128]{2,1,0:T(2,128)(2,1)S(1)}, bf16[64,2,128]{2,1,0:T(2,128)(2,1)}, u32[]{:S(2)}) copy-start(bf16[64,2,128]{2,1,0:T(2,128)(2,1)} %param.9) | copy-start | bytes 98308

commit v6 on v5

--- a/solution.py
+++ b/solution.py
@@ -303,7 +303,11 @@
     def exact(onehot, values):
         high = values.astype(BF16)
         low = (values - high.astype(F32)).astype(BF16)
-        return jnp.dot(onehot, high, preferred_element_type=F32) + jnp.dot(onehot, low, preferred_element_type=F32)
+        return jnp.dot(
+            jnp.concatenate([onehot, onehot], axis=1),
+            jnp.concatenate([high, low], axis=0),
+            preferred_element_type=F32,
+        )
 
     sent = exact(gather, prod[...])
     last = lax.broadcasted_iota(I32, (MSG, BLK), 0) == CAP

time: 23.9 us -> 23.9 us (level)
  no operation moved by 1% of the time
where the time goes in v6:
time: 23.9 us; the launch traced here: 23.7 us
  Pallas kernels  22.3 us (93%)
  between operations  0.78 us (3%)
  local copies, waits for them, and re-layouts  0.68 us (3%)
    pallas_call x1, Pallas kernels, call(): pl.pallas_call(fn, out_shape=shapes, in_specs=[pl.BlockSpec(memory_space=...  22.3 us
    unnamed x11, local copies, waits for them, and re-layouts  0.68 us

profile of v6, /device:TPU:1, one launch (start us, length us, event | category | flops | bytes accessed | tf_op | source)
XLA Modules:
  0.0 23.7 jit_solution(2440467034054225516)
XLA Ops:
  0.0 0.0 copy-start.1
  0.0 0.0 copy-start.2
  0.0 0.0 copy-start.4
  0.0 0.0 copy-start.3
  0.0 0.0 copy-start
  0.7 22.3 %shard_map.75 = (f32[16,2048]{1,0:T(8,128)S(1)}, s32[1,1]{1,0:T(1,128)S(4)}) custom-call(bf16[128,128]{1,0:T(8,128)(2,1)} %bitcast.11, bf16[128,128,128]{2,1,0:T(8,128)(2,1)} %bitcast.9, f32[1,64]{1,0:T(1,128)} %bitcast.18, s32[1,64]{1,0:T(1,128)} %bitcast.20, s32[2,64]{1,0:T(2,128)} %bitcast.16, s32[1,1]{1,0:T(1,128)} %bitcast.8.counts_h, s32[256]{0:T(256)} %owners_h.1, ...), custom_call_target="tpu_custom_call" | custom-call | tf_op jit(solution)/shard_map/pallas_call | solution.py:447
  23.0 0.0 copy-done.1
  23.0 0.0 copy-done.2
  23.0 0.0 copy-done.4
  23.1 0.0 copy-done.3
  23.1 0.0 copy-done
  23.1 0.7 %copy.13 = f32[16,2048]{1,0:T(8,128)} copy(f32[16,2048]{1,0:T(8,128)S(1)} %get-tuple-element.37) | data formatting | bytes 262144
  (1 shorter events, 0.0 us)
Async XLA Ops:
  0.0 23.0 %copy-start.1 = (s32[256]{0:T(256)S(1)}, s32[256]{0:T(256)}, u32[]{:S(2)}) copy-start(s32[256]{0:T(256)} %owners_h.1) | copy-start | bytes 3076
  0.0 23.0 %copy-start.2 = (s32[64,2]{0,1:T(2,128)S(1)}, s32[64,2]{0,1:T(2,128)}, u32[]{:S(2)}) copy-start(s32[64,2]{0,1:T(2,128)} %param.13) | copy-start | bytes 1540
  0.0 23.0 %copy-start.4 = (s32[64]{0:T(128)S(1)}, s32[64]{0:T(128)}, u32[]{:S(2)}) copy-start(s32[64]{0:T(128)} %param.12) | copy-start | bytes 772
  0.0 23.0 %copy-start.3 = (f32[64]{0:T(128)S(1)}, f32[64]{0:T(128)}, u32[]{:S(2)}) copy-start(f32[64]{0:T(128)} %param.11) | copy-start | bytes 772
  0.0 23.0 %copy-start = (bf16[64,2,128]{2,1,0:T(2,128)(2,1)S(1)}, bf16[64,2,128]{2,1,0:T(2,128)(2,1)}, u32[]{:S(2)}) copy-start(bf16[64,2,128]{2,1,0:T(2,128)(2,1)} %param.9) | copy-start | bytes 98308
